TPU v7x, 32 devices: a whole 2x2x4 slice. The times are simulated.
32 devices in a mesh: blk: 8 (over z, y), col: 4 (over x, core).
Axes of the slice: x: 2, y: 2, z: 4, core: 2. Of those that a mesh axis runs over, the one named last changes fastest.
Arguments:
- amplitudes: float32 [800, 32, 1601], P('col', 'blk'), may hold values from -6 to 6
- integrals: float32 [2, 1024, 20, 1601], P(None, 'blk', 'col'), may hold values from -0.03125 to 0.03125
- block_ids: int32 [20], replicated, may hold values from 0 to 799, as said below
- mirror: int32 [16], replicated, may hold values from 0 to 15, each once
Outputs:
- ladder_residual: float32 [16, 1024], P('col', 'blk')
Inputs may be any that keep to these rules, and one draw needn't show every extreme that they name: `block_ids`: 20 distinct folded block numbers; 0 and 799 are always among them. `mirror`: a permutation of the slab positions.
All inputs are finite; a program needn't handle non-finite values.
Results may differ from a plain program's by a relative error of at most 0.000073.
Values sent between devices are 32-bit elements; how exact they have to be, the bound alone decides.
A program may use at most 64 MiB of HBM per device.

v0:
```python
import jax
import jax.numpy as jnp
from jax import lax
from jax.sharding import PartitionSpec as P


def body(amplitudes, integrals, block_ids, mirror):
    blocks_here = amplitudes.shape[0]
    block_width = amplitudes.shape[2]
    owned_count = integrals.shape[2]
    local_rows = integrals.shape[1]
    block_base = lax.axis_index("col") * blocks_here
    stacked = integrals.reshape(2 * local_rows, owned_count, block_width)
    wanted = block_ids - block_base
    onehot = (wanted[:, None] == jnp.arange(blocks_here, dtype=jnp.int32)[None, :]).astype(
        jnp.float32
    )
    selected = lax.psum_scatter(
        jnp.einsum("kh,hrl->krl", onehot, amplitudes, precision=lax.Precision.HIGHEST),
        "col",
        scatter_dimension=0,
        tiled=True,
    )
    products = jnp.einsum(
        "kcl,wkl->cw",
        lax.all_gather(selected, "blk", axis=1, tiled=True),
        stacked,
        precision=lax.Precision.HIGHEST,
    )
    pair_count = products.shape[0] // 2
    plus_part = products[:, :local_rows]
    minus_part = products[:, local_rows:]
    direct = 0.5 * (
        plus_part[:pair_count]
        + minus_part[:pair_count]
        + plus_part[pair_count:]
        - minus_part[pair_count:]
    )
    swapped = 0.5 * (
        plus_part[:pair_count]
        - minus_part[:pair_count]
        + plus_part[pair_count:]
        + minus_part[pair_count:]
    )
    direct_sum, swapped_sum = (
        lax.psum_scatter(direct, "col", scatter_dimension=0, tiled=True),
        lax.psum_scatter(swapped, "col", scatter_dimension=0, tiled=True),
    )
    swapped_all = lax.all_gather(swapped_sum, "col", axis=0, tiled=True)
    own_pairs = direct_sum.shape[0]
    targets = lax.dynamic_slice_in_dim(mirror, lax.axis_index("col") * own_pairs, own_pairs)
    pick = (targets[:, None] == jnp.arange(pair_count, dtype=jnp.int32)[None, :]).astype(
        jnp.float32
    )
    return direct_sum + jnp.dot(pick, swapped_all, precision=lax.Precision.HIGHEST)


def solution(mesh):
    in_specs = (P("col", "blk", None), P(None, "blk", "col", None), P(), P())
    out_specs = P("col", "blk")
    return jax.shard_map(body, mesh=mesh, in_specs=in_specs, out_specs=out_specs, check_vma=False)
```

profile of v0, /device:TPU:0, one launch (start us, length us, event | category | flops | bytes accessed | tf_op | source)
XLA Modules:
  0.0 118.5 jit_solution(15536446643626224223)
XLA Ops:
  6.5 0.0 copy-start.1
  6.5 0.0 all-reduce.6.cloned.1.call-start
  6.5 0.7 broadcast_subtract_fusion
  7.2 4.3 %fusion = f32[20,4,1601]{2,0,1:T(8,128)S(1)} fusion(f32[200,4,1601]{2,1,0:T(4,128)} %param.4, s32[20]{0:T(128)S(1)} %broadcast_subtract_fusion), kind=kOutput, calls=%fused_computation | convolution fusion | flops 307396000 | bytes 5635600 | tf_op jit(solution)/shard_map/kh,hrl->krl/dot_general | solution.py:19
  11.6 1.0 copy.8
  12.6 0.0 all-reduce.6.cloned.1.call-update
  12.6 0.0 copy-done.1
  12.6 0.6 dynamic-slice
  14.5 0.0 copy-start
  14.5 10.6 %reshape.5 = f32[256,5,1601]{0,2,1:T(8,128)} reshape(f32[2,128,5,1601]{1,0,3,2:T(2,128)} %param.5) | data formatting | bytes 16394240 | tf_op jit(solution)/shard_map/reshape | solution.py:13
  25.1 0.0 copy-done
  25.1 0.1 dynamic_slice.3
  25.2 23.6 %all-reduce.6.cloned.1.call-done = f32[20,4,1601]{2,1,0:T(4,128)} async-done(((f32[20,4,1601]{2,1,0:T(4,128)}), f32[20,4,1601]{2,1,0:T(4,128)}) %all-reduce.6.cloned.1.call-update) | async-done | bytes 512336
  48.8 0.9 constant_dynamic-slice_fusion
  49.7 38.5 %all_gather.6 = f32[5,32,1601]{2,0,1:T(8,128)S(1)} all-gather(f32[5,4,1601]{2,0,1:T(8,128)S(1)} %copy.5), channel_id=1, replica_groups=mesh['blk'=8,'col'=4] {'blk'}, dimensions={1}, use_global_device_ids=true | all-gather | bytes 1152720 | tf_op jit(solution)/shard_map/all_gather | solution.py:26
  88.3 7.3 %convolution_bitcast_fusion = f32[32,256]{1,0:T(8,128)S(1)} fusion(f32[256,5,1601]{0,2,1:T(8,128)} %reshape.5, f32[5,32,1601]{2,0,1:T(8,128)S(1)} %all_gather.6), kind=kOutput, calls=%fused_computation.2 | convolution fusion | flops 786923520 | bytes 9254528 | tf_op jit(solution)/shard_map/kcl,wkl->cw/dot_general | solution.py:24
  95.6 10.1 %all-reduce.3 = (f32[16,128]{1,0:T(8,128)S(1)}, f32[16,128]{1,0:T(8,128)S(1)}) all-reduce(f32[16,128]{1,0:T(8,128)S(1)} %get-tuple-element.8, f32[16,128]{1,0:T(8,128)S(1)} %get-tuple-element.7), channel_id=4, replica_groups=mesh['blk'=8,'col'=4] {'col'}, use_global_device_ids=true, to_apply=%region_2.0.clone | all-reduce | flops 4096 | bytes 32768
  105.7 5.2 %all-gather = f32[4,4,128]{2,1,0:T(4,128)S(1)} all-gather(f32[1,4,128]{2,1,0:T(4,128)S(1)} %dynamic-slice_bitcast_fusion), channel_id=1, replica_groups=mesh['blk'=8,'col'=4] {'col'}, dimensions={0}, use_global_device_ids=true | all-gather | bytes 10240 | tf_op jit(solution)/shard_map/all_gather | solution.py:49
  110.9 0.8 convolution_add_fusion
  (3 shorter events, 0.0 us)
Async XLA Ops:
  6.5 6.1 %copy-start.1 = (u32[32]{0:T(128)S(1)}, u32[32]{0:T(128)}, u32[]{:S(2)}) copy-start(u32[32]{0:T(128)} %constant.18) | copy-start | bytes 388
  6.5 42.3 %all-reduce.6.cloned.1.call-start = ((), (), s32[]{:S(2)}) async-start(), calls=%async_computation | async-start | bytes 1064960
  14.5 10.7 %copy-start = (s32[16]{0:T(128)S(1)}, s32[16]{0:T(128)}, u32[]{:S(2)}) copy-start(s32[16]{0:T(128)} %param.7) | copy-start | bytes 196
Sparse Core Ops, SparseCore 0:
  12.7 36.0 all-reduce.5
where the time goes:
time: 119 us
  blocking collectives  53.9 us (45%)
  waiting for transfers between devices  23.6 us (20%)
  between operations  14.7 us (12%)
  local copies, waits for them, and re-layouts  13.3 us (11%)
  matrix products  12.4 us (10%)
    all_gather x1, blocking collectives, body(): lax.all_gather(selected, 'blk', axis=1, tiled=True)  38.5 us
    unnamed x2, waiting for transfers between devices  23.6 us
    reshape x1, local copies, waits for them, and re-layouts, body(): stacked = integrals.reshape(2 * local_rows, owned_count, block_width)  10.6 us
    unnamed x1, blocking collectives  10.1 us
    dot_general x1, matrix products, body(): jnp.einsum('kcl,wkl->cw', lax.all_gather(selected, 'blk', axis=1, tiled=T...  7.29 us
    all_gather x1, blocking collectives, body(): swapped_all = lax.all_gather(swapped_sum, 'col', axis=0, tiled=True)  5.19 us
    dot_general x1, matrix products, body(): jnp.einsum('kh,hrl->krl', onehot, amplitudes, precision=lax.Precision.HIG...  4.35 us
  transfers between devices with their start and end apart: 1, of which 1 were waited for; matrix products, arithmetic and copies ran while one was open for 10% of the time, Pallas kernels for 0%

commit v1 on v0

v1 whole, which is shorter than its diff:
```python
import functools

import jax
import jax.numpy as jnp
from jax import lax
from jax.experimental import pallas as pl
from jax.experimental.pallas import tpu as pltpu
from jax.sharding import PartitionSpec as P

MESH = pl.DeviceIdType.MESH


def kernel(
    nblk, ncol,
    amp_hbm, int_hbm, ids, mirror, out_ref,
    amp_v, int_v, hi, lo, sendb, landed, gath, feed, swp, osend, orecv,
    amp_sem, int_sem, xs, xr, us, ds, ys, gr, os_, or_,
):
    blocks_here = amp_v.shape[0]
    own = int_v.shape[0]
    rows = amp_v.shape[1]
    width = amp_v.shape[2]
    ab = int_v.shape[2]
    padded = hi.shape[1]
    pairs = feed.shape[0] // 2
    own_pairs = osend.shape[1]
    nhi = nblk // 2
    half = nblk // 2
    b = lax.axis_index("blk")
    c = lax.axis_index("col")
    z = b // 2
    y = b % 2
    partner = z * 2 + (1 - y)

    amp_copy = pltpu.make_async_copy(amp_hbm, amp_v, amp_sem)
    amp_copy.start()
    int_copies = {}
    for k in range(own):
        cp = pltpu.make_async_copy(int_hbm.at[k], int_v.at[k].reshape(width, 2, ab), int_sem.at[k])
        cp.start()
        int_copies[k] = cp

    barrier = pltpu.get_barrier_semaphore()
    for j in range(1, ncol):
        pl.semaphore_signal(barrier, inc=1, device_id=(b, (c + j) % ncol), device_id_type=MESH)
    pl.semaphore_signal(barrier, inc=1, device_id=(partner, c), device_id_type=MESH)

    @pl.when(z < nhi - 1)
    def _():
        pl.semaphore_signal(barrier, inc=1, device_id=(b + 2, c), device_id_type=MESH)

    @pl.when(z > 0)
    def _():
        pl.semaphore_signal(barrier, inc=1, device_id=(b - 2, c), device_id_type=MESH)

    ends = (z == 0).astype(jnp.int32) + (z == nhi - 1).astype(jnp.int32)
    pl.semaphore_wait(barrier, ncol + 2 - ends)

    def xcopy(k, j):
        return pltpu.make_async_remote_copy(
            src_ref=sendb.at[j, k], dst_ref=landed.at[j, k],
            send_sem=xs.at[j, k], recv_sem=xr.at[j, k],
            device_id=(b, (c + j) % ncol), device_id_type=MESH)

    def gcopy(k, src, sem, target):
        return pltpu.make_async_remote_copy(
            src_ref=gath.at[k, src], dst_ref=gath.at[k, src],
            send_sem=sem, recv_sem=gr.at[k, src],
            device_id=(target, c), device_id_type=MESH)

    def up(k, d):
        return gcopy(k, b - 2 * d, us.at[k, d], b + 2)

    def down(k, d):
        return gcopy(k, b + 2 * d, ds.at[k, d], b - 2)

    def across(k, zz):
        return gcopy(k, zz * 2 + y, ys.at[k, zz], partner)

    def arrived(k, src):
        gcopy(k, src, us.at[k, 0], partner).wait_recv()

    base = c * blocks_here

    def wanted(k, dest):
        here = ids[dest * own + k] - base
        ok = jnp.logical_and(here >= 0, here < blocks_here)
        at = jnp.minimum(jnp.maximum(here, 0), blocks_here - 1)
        return jnp.where(ok, amp_v[at], 0.0)

    amp_copy.wait()
    for k in range(own):
        for j in range(1, ncol):
            sendb[j, k] = wanted(k, (c + j) % ncol)
            xcopy(k, j).start()
    for k in range(own):
        sendb[0, k] = wanted(k, c)

    tail = (width // 128) * 128
    if padded > width:
        feed[:, tail:] = jnp.zeros((2 * pairs, padded - tail), jnp.float32)

    def convert(k):
        int_copies[k].wait()
        whole = width // 16

        def split(at, count):
            for w in range(2):
                v = int_v[k, pl.ds(at * 2 + w, count, stride=2), :]
                h = v.astype(jnp.bfloat16)
                l = (v - h.astype(jnp.float32)).astype(jnp.bfloat16)
                if count < 16:
                    blank = jnp.zeros((16 - count, ab), jnp.bfloat16)
                    h = jnp.concatenate([h, blank], axis=0)
                    l = jnp.concatenate([l, blank], axis=0)
                hi[k, pl.ds(at, 16), w * ab:(w + 1) * ab] = h
                lo[k, pl.ds(at, 16), w * ab:(w + 1) * ab] = l

        def strip(i, carry):
            split(pl.multiple_of(i * 16, 16), 16)
            return carry

        lax.fori_loop(0, whole, strip, 0, unroll=4)
        end = whole * 16
        if width > end:
            split(end, width - end)
            end += 16
        if padded > end:
            hi[k, end:] = jnp.zeros((padded - end, 2 * ab), jnp.bfloat16)
            lo[k, end:] = jnp.zeros((padded - end, 2 * ab), jnp.bfloat16)

    def own_piece(k):
        for j in range(1, ncol):
            xcopy(k, j).wait_recv()
        total = sendb[0, k]
        for j in range(1, ncol):
            total = total + landed[j, k]
        gath[k, b] = total
        across(k, z).start()

        @pl.when(z < nhi - 1)
        def _():
            up(k, 0).start()

        @pl.when(z > 0)
        def _():
            down(k, 0).start()

    def relay(k, d):
        @pl.when(z >= d)
        def _():
            arrived(k, b - 2 * d)

            @pl.when(z < nhi - 1)
            def _():
                up(k, d).start()

            across(k, z - d).start()

        @pl.when(z + d < nhi)
        def _():
            arrived(k, b + 2 * d)

            @pl.when(z > 0)
            def _():
                down(k, d).start()

            across(k, z + d).start()

    def multiply(k, acc):
        for zz in range(nhi):
            arrived(k, zz * 2 + 1 - y)
        for i in range(half):
            first = gath[k, i]
            second = gath[k, half + i]
            feed[i * rows:(i + 1) * rows, :width] = first + second
            feed[pairs + i * rows:pairs + (i + 1) * rows, :width] = first - second
        f = feed[...]
        fh = f.astype(jnp.bfloat16)
        fl = (f - fh.astype(jnp.float32)).astype(jnp.bfloat16)
        both = jnp.concatenate([fh, fl], axis=0)
        big = jnp.dot(both, hi[k], preferred_element_type=jnp.float32)
        small = jnp.dot(fh, lo[k], preferred_element_type=jnp.float32)
        part = big[:2 * pairs] + (big[2 * pairs:] + small)
        new = [part[:pairs, :ab], part[pairs:, ab:]]
        return new if acc is None else [u + v for u, v in zip(acc, new)]

    convert(0)
    for t in range(own + nhi - 1):
        if t < own:
            own_piece(t)
            if t + 1 < own:
                convert(t + 1)
        for d in range(1, nhi):
            k = t - d
            if 0 <= k < own:
                relay(k, d)
    acc = None
    for k in range(own):
        acc = multiply(k, acc)

    x_part, y_part = acc
    swp[...] = 0.5 * (x_part - y_part)
    direct = 0.5 * (x_part + y_part)
    for q in range(ncol):
        for i in range(own_pairs):
            p = q * own_pairs + i
            osend[q, i:i + 1, :] = direct[p:p + 1] + swp[pl.ds(mirror[p], 1), :]

    def ocopy(j):
        dest = (c + j) % ncol
        return pltpu.make_async_remote_copy(
            src_ref=osend.at[dest], dst_ref=orecv.at[j],
            send_sem=os_.at[j], recv_sem=or_.at[j],
            device_id=(b, dest), device_id_type=MESH)

    for j in range(1, ncol):
        ocopy(j).start()
    total = osend[c]
    for j in range(1, ncol):
        ocopy(j).wait_recv()
    for j in range(1, ncol):
        total = total + orecv[j]
    out_ref[...] = total

    for j in range(1, ncol):
        ocopy(j).wait_send()
        for k in range(own):
            xcopy(k, j).wait_send()
    for k in range(own):
        for zz in range(nhi):
            across(k, zz).wait_send()
        for d in range(nhi):
            @pl.when(jnp.logical_and(z >= d, z < nhi - 1))
            def _():
                up(k, d).wait_send()

            @pl.when(jnp.logical_and(z + d < nhi, z > 0))
            def _():
                down(k, d).wait_send()


def body(nblk, ncol, amplitudes, integrals, block_ids, mirror):
    blocks_here, rows, width = amplitudes.shape
    _, ab, own, _ = integrals.shape
    pairs = mirror.shape[0]
    own_pairs = pairs // ncol
    padded = -(-width // 128) * 128
    nhi = nblk // 2
    f32 = jnp.float32
    dma = pltpu.SemaphoreType.DMA
    return pl.pallas_call(
        functools.partial(kernel, nblk, ncol),
        out_shape=jax.ShapeDtypeStruct((own_pairs, ab), f32),
        in_specs=[
            pl.BlockSpec(memory_space=pl.ANY),
            pl.BlockSpec(memory_space=pl.ANY),
            pl.BlockSpec(memory_space=pltpu.SMEM),
            pl.BlockSpec(memory_space=pltpu.SMEM),
        ],
        out_specs=pl.BlockSpec(memory_space=pltpu.VMEM),
        scratch_shapes=[
            pltpu.VMEM((blocks_here, rows, width), f32),
            pltpu.VMEM((own, 2 * width, ab), f32),
            pltpu.VMEM((own, padded, 2 * ab), jnp.bfloat16),
            pltpu.VMEM((own, padded, 2 * ab), jnp.bfloat16),
            pltpu.VMEM((ncol, own, rows, width), f32),
            pltpu.VMEM((ncol, own, rows, width), f32),
            pltpu.VMEM((own, nblk, rows, width), f32),
            pltpu.VMEM((2 * pairs, padded), f32),
            pltpu.VMEM((pairs, ab), f32),
            pltpu.VMEM((ncol, own_pairs, ab), f32),
            pltpu.VMEM((ncol, own_pairs, ab), f32),
            dma(()),
            dma((own,)),
            dma((ncol, own)),
            dma((ncol, own)),
            dma((own, nhi)),
            dma((own, nhi)),
            dma((own, nhi)),
            dma((own, nblk)),
            dma((ncol,)),
            dma((ncol,)),
        ],
        compiler_params=pltpu.CompilerParams(
            collective_id=0, has_side_effects=True, vmem_limit_bytes=60 * 1024 * 1024
        ),
    )(amplitudes, jnp.transpose(integrals, (2, 3, 0, 1)), block_ids, mirror)


def solution(mesh):
    in_specs = (P("col", "blk", None), P(None, "blk", "col", None), P(), P())
    out_specs = P("col", "blk")
    call = functools.partial(body, mesh.shape["blk"], mesh.shape["col"])
    return jax.shard_map(call, mesh=mesh, in_specs=in_specs, out_specs=out_specs, check_vma=False)
```

time: 119 us -> 37.3 us (0.31)
  blocking collectives: 53.9 us -> 0 us
  Pallas kernels: 0 us -> 35.9 us
  waiting for transfers between devices: 23.6 us -> 0 us
  between operations: 14.7 us -> 0.01 us
  matrix products: 12.4 us -> 0 us
  local copies, waits for them, and re-layouts: 13.3 us -> 1.26 us
    all_gather x2 -> x0, blocking collectives: 43.7 us -> none  [the longest x1 38.5 us: body(): lax.all_gather(selected, 'blk', axis=1, tiled=True)]
    pallas_call x0 -> x1, Pallas kernels: none -> 35.9 us  [body(): pl.pallas_call(functools.partial(kernel, nblk, ncol), out_shape=jax.Shape...]
    unnamed x2 -> x0, waiting for transfers between devices: 23.6 us -> none
    dot_general x3 -> x0, matrix products: 12.4 us -> none  [the longest x1 7.29 us: body(): jnp.einsum('kcl,wkl->cw', lax.all_gather(selected, 'blk', axis=1, tiled=T...]
    reshape x1 -> x0, local copies, waits for them, and re-layouts: 10.6 us -> none  [body(): stacked = integrals.reshape(2 * local_rows, owned_count, block_width)]
    unnamed x1 -> x0, blocking collectives: 10.1 us -> none
  transfers between devices with their start and end apart: 1 -> 0, of which waited for: 1 -> 0; matrix products, arithmetic and copies ran while one was open for 10% -> 0% of each run, Pallas kernels for 0% -> 0%
where the time goes in v1:
time: 37.3 us; the launch traced here: 37.2 us
  Pallas kernels  35.9 us (96%)
  local copies, waits for them, and re-layouts  1.26 us (3%)
    pallas_call x1, Pallas kernels, body(): pl.pallas_call(functools.partial(kernel, nblk, ncol), out_shape=jax.Shape...  35.9 us
    unnamed x1, local copies, waits for them, and re-layouts  1.26 us

profile of v1, /device:TPU:0, one launch (start us, length us, event | category | flops | bytes accessed | tf_op | source)
XLA Modules:
  0.0 37.2 jit_solution(7650445626445988265)
XLA Ops:
  0.0 35.9 %shard_map.46 = f32[4,128]{1,0:T(4,128)} custom-call(f32[200,4,1601]{2,1,0:T(4,128)} %amp_hbm.1, f32[5,1601,2,128]{3,2,1,0:T(2,128)} %bitcast.1, s32[20]{0:T(128)} %ids.1, s32[16]{0:T(128)} %mirror.1), custom_call_target="tpu_custom_call" | custom-call | tf_op jit(solution)/shard_map/pallas_call | solution.py:252
  35.9 1.3 %copy.6 = f32[4,128]{1,0:T(4,128)} copy(f32[4,128]{1,0:T(4,128)} %shard_map.46) | data formatting | bytes 4096

commit v2 on v1

--- a/solution.py
+++ b/solution.py
@@ -13,8 +13,8 @@
 def kernel(
     nblk, ncol,
     amp_hbm, int_hbm, ids, mirror, out_ref,
-    amp_v, int_v, hi, lo, sendb, landed, gath, feed, swp, osend, orecv,
-    amp_sem, int_sem, xs, xr, us, ds, ys, gr, os_, or_,
+    amp_v, int_v, hi, lo, core_out, core_in, sendb, landed, gath, feed, swp, osend, orecv,
+    amp_sem, int_sem, cs, cr, xs, xr, us, ds, ys, gr, os_, or_,
 ):
     blocks_here = amp_v.shape[0]
     own = int_v.shape[0]
@@ -30,16 +30,18 @@
     c = lax.axis_index("col")
     z = b // 2
     y = b % 2
+    nx = ncol // 2
+    x = c // 2
+    q = c % 2
     partner = z * 2 + (1 - y)
 
-    amp_copy = pltpu.make_async_copy(amp_hbm, amp_v, amp_sem)
-    amp_copy.start()
-    int_copies = {}
-    for k in range(own):
-        cp = pltpu.make_async_copy(int_hbm.at[k], int_v.at[k].reshape(width, 2, ab), int_sem.at[k])
+    amp_copies = []
+    for i in range(4):
+        low, high = blocks_here * i // 4, blocks_here * (i + 1) // 4
+        cp = pltpu.make_async_copy(
+            amp_hbm.at[low:high], amp_v.at[low:high], amp_sem.at[i])
         cp.start()
-        int_copies[k] = cp
-
+        amp_copies.append(cp)
     barrier = pltpu.get_barrier_semaphore()
     for j in range(1, ncol):
         pl.semaphore_signal(barrier, inc=1, device_id=(b, (c + j) % ncol), device_id_type=MESH)
@@ -56,11 +58,17 @@
     ends = (z == 0).astype(jnp.int32) + (z == nhi - 1).astype(jnp.int32)
     pl.semaphore_wait(barrier, ncol + 2 - ends)
 
-    def xcopy(k, j):
+    def core_copy(k, i):
         return pltpu.make_async_remote_copy(
-            src_ref=sendb.at[j, k], dst_ref=landed.at[j, k],
-            send_sem=xs.at[j, k], recv_sem=xr.at[j, k],
-            device_id=(b, (c + j) % ncol), device_id_type=MESH)
+            src_ref=core_out.at[i, k], dst_ref=core_in.at[i, k],
+            send_sem=cs.at[i, k], recv_sem=cr.at[i, k],
+            device_id=(b, x * 2 + 1 - q), device_id_type=MESH)
+
+    def xcopy(k, i):
+        return pltpu.make_async_remote_copy(
+            src_ref=sendb.at[i, k], dst_ref=landed.at[i, k],
+            send_sem=xs.at[i, k], recv_sem=xr.at[i, k],
+            device_id=(b, (x + i) % nx * 2 + q), device_id_type=MESH)
 
     def gcopy(k, src, sem, target):
         return pltpu.make_async_remote_copy(
@@ -88,13 +96,24 @@
         at = jnp.minimum(jnp.maximum(here, 0), blocks_here - 1)
         return jnp.where(ok, amp_v[at], 0.0)
 
-    amp_copy.wait()
-    for k in range(own):
-        for j in range(1, ncol):
-            sendb[j, k] = wanted(k, (c + j) % ncol)
-            xcopy(k, j).start()
-    for k in range(own):
-        sendb[0, k] = wanted(k, c)
+    for cp in amp_copies:
+        cp.wait()
+    int_copies = {}
+    for k in range(own):
+        cp = pltpu.make_async_copy(int_hbm.at[k], int_v.at[k].reshape(width, 2, ab), int_sem.at[k])
+        cp.start()
+        int_copies[k] = cp
+
+    for k in range(own):
+        for i in [*range(1, nx), 0]:
+            core_out[i, k] = wanted(k, (x + i) % nx * 2 + 1 - q)
+            core_copy(k, i).start()
+    for k in range(own):
+        for i in range(1, nx):
+            mine = wanted(k, (x + i) % nx * 2 + q)
+            core_copy(k, i).wait_recv()
+            sendb[i, k] = mine + core_in[i, k]
+            xcopy(k, i).start()
 
     tail = (width // 128) * 128
     if padded > width:
@@ -130,11 +149,12 @@
             lo[k, end:] = jnp.zeros((padded - end, 2 * ab), jnp.bfloat16)
 
     def own_piece(k):
-        for j in range(1, ncol):
-            xcopy(k, j).wait_recv()
-        total = sendb[0, k]
-        for j in range(1, ncol):
-            total = total + landed[j, k]
+        total = wanted(k, c)
+        core_copy(k, 0).wait_recv()
+        total = total + core_in[0, k]
+        for i in range(1, nx):
+            xcopy(k, i).wait_recv()
+            total = total + landed[i, k]
         gath[k, b] = total
         across(k, z).start()
 
@@ -185,16 +205,17 @@
         new = [part[:pairs, :ab], part[pairs:, ab:]]
         return new if acc is None else [u + v for u, v in zip(acc, new)]
 
+    events = sorted((k * 1 + d * 100, d, k) for k in range(own) for d in range(nhi))
     convert(0)
-    for t in range(own + nhi - 1):
-        if t < own:
-            own_piece(t)
-            if t + 1 < own:
-                convert(t + 1)
-        for d in range(1, nhi):
-            k = t - d
-            if 0 <= k < own:
-                relay(k, d)
+    ready = 1
+    for _, d, k in events:
+        if d == 0:
+            own_piece(k)
+        else:
+            relay(k, d)
+        if ready < own:
+            convert(ready)
+            ready += 1
     acc = None
     for k in range(own):
         acc = multiply(k, acc)
@@ -202,10 +223,10 @@
     x_part, y_part = acc
     swp[...] = 0.5 * (x_part - y_part)
     direct = 0.5 * (x_part + y_part)
-    for q in range(ncol):
+    for g in range(ncol):
         for i in range(own_pairs):
-            p = q * own_pairs + i
-            osend[q, i:i + 1, :] = direct[p:p + 1] + swp[pl.ds(mirror[p], 1), :]
+            p = g * own_pairs + i
+            osend[g, i:i + 1, :] = direct[p:p + 1] + swp[pl.ds(mirror[p], 1), :]
 
     def ocopy(j):
         dest = (c + j) % ncol
@@ -225,9 +246,11 @@
 
     for j in range(1, ncol):
         ocopy(j).wait_send()
-        for k in range(own):
-            xcopy(k, j).wait_send()
-    for k in range(own):
+    for k in range(own):
+        for i in range(nx):
+            core_copy(k, i).wait_send()
+        for i in range(1, nx):
+            xcopy(k, i).wait_send()
         for zz in range(nhi):
             across(k, zz).wait_send()
         for d in range(nhi):
@@ -247,6 +270,7 @@
     own_pairs = pairs // ncol
     padded = -(-width // 128) * 128
     nhi = nblk // 2
+    nx = ncol // 2
     f32 = jnp.float32
     dma = pltpu.SemaphoreType.DMA
     return pl.pallas_call(
@@ -264,17 +288,21 @@
             pltpu.VMEM((own, 2 * width, ab), f32),
             pltpu.VMEM((own, padded, 2 * ab), jnp.bfloat16),
             pltpu.VMEM((own, padded, 2 * ab), jnp.bfloat16),
-            pltpu.VMEM((ncol, own, rows, width), f32),
-            pltpu.VMEM((ncol, own, rows, width), f32),
+            pltpu.VMEM((nx, own, rows, width), f32),
+            pltpu.VMEM((nx, own, rows, width), f32),
+            pltpu.VMEM((nx, own, rows, width), f32),
+            pltpu.VMEM((nx, own, rows, width), f32),
             pltpu.VMEM((own, nblk, rows, width), f32),
             pltpu.VMEM((2 * pairs, padded), f32),
             pltpu.VMEM((pairs, ab), f32),
             pltpu.VMEM((ncol, own_pairs, ab), f32),
             pltpu.VMEM((ncol, own_pairs, ab), f32),
-            dma(()),
+            dma((4,)),
             dma((own,)),
-            dma((ncol, own)),
-            dma((ncol, own)),
+            dma((nx, own)),
+            dma((nx, own)),
+            dma((nx, own)),
+            dma((nx, own)),
             dma((own, nhi)),
             dma((own, nhi)),
             dma((own, nhi)),

time: 37.3 us -> 31.6 us (0.85)
  Pallas kernels: 35.9 us -> 30.1 us
    pallas_call x1, Pallas kernels: 35.9 us -> 30.1 us  [body(): pl.pallas_call(functools.partial(kernel, nblk, ncol), out_shape=jax.Shape...]
where the time goes in v2:
time: 31.6 us; the launch traced here: 31.4 us
  Pallas kernels  30.1 us (95%)
  local copies, waits for them, and re-layouts  1.26 us (4%)
    pallas_call x1, Pallas kernels, body(): pl.pallas_call(functools.partial(kernel, nblk, ncol), out_shape=jax.Shape...  30.1 us
    unnamed x1, local copies, waits for them, and re-layouts  1.26 us

profile of v2, /device:TPU:0, one launch (start us, length us, event | category | flops | bytes accessed | tf_op | source)
XLA Modules:
  0.0 31.4 jit_solution(3792903572823973991)
XLA Ops:
  0.0 30.1 %shard_map.46 = f32[4,128]{1,0:T(4,128)} custom-call(f32[200,4,1601]{2,1,0:T(4,128)} %amp_hbm.1, f32[5,1601,2,128]{3,2,1,0:T(2,128)} %bitcast.1, s32[20]{0:T(128)} %ids.1, s32[16]{0:T(128)} %mirror.1), custom_call_target="tpu_custom_call" | custom-call | tf_op jit(solution)/shard_map/pallas_call | solution.py:276
  30.1 1.3 %copy.6 = f32[4,128]{1,0:T(4,128)} copy(f32[4,128]{1,0:T(4,128)} %shard_map.46) | data formatting | bytes 4096
